TPU v7x, 32 devices: a whole 2x2x4 slice. The times are simulated.
32 devices in a mesh: src: 4 (over y, core), help: 8 (over z, x).
Axes of the slice: x: 2, y: 2, z: 4, core: 2. Of those that a mesh axis runs over, the one named last changes fastest.
Arguments:
- tiles: int32 [2, 256], P(None, 'src'), may hold values from 0 to 31, as said below
- cell_slot: int32 [2, 32], replicated, may hold values from 0 to 31, as said below
- counts: int32 [32, 2], P(('src', 'help')), may hold values from 128 to 512, as said below
- src_points: bfloat16 [16384, 512], P(('src', 'help')), may hold values from -9 to 9
- tgt_points: bfloat16 [16384, 512], P(('src', 'help')), may hold values from -9 to 9
Outputs:
- source_potential: float32 [16384], P(('src', 'help'))
- target_potential: float32 [16384], P(('src', 'help'))
- transport: float32 [16384, 512], P(('src', 'help'))
Inputs may be any that keep to these rules, and one draw needn't show every extreme that they name: `tiles`: columns come in blocks of 64, block g for group g of 8 cells: a block's source cells have ids g * 8 to g * 8 + 7, its target cells lie in group g or in group g + 1 (group 4 - 1 is followed by group 0); no pair is listed twice, and every source cell and every target cell is named in some column. Each row is a permutation that keeps every cell in its group: cell c is stored at slot cell_slot[side, c], with cell_slot[side, c] // 8 equal to c // 8; slot k is rows k * 512 to k * 512 + 511 of the point arrays. `counts`: rows of a slot at and beyond its count are padding. Both ends of the range occur in each column.
All inputs are finite; a program needn't handle non-finite values.
Results may differ from a plain program's by a relative error of at most 0.004.
Values may be sent and summed in bfloat16 or wider, within the bound.
A program may use at most 192 MiB of HBM per device.

v0:
```python
import math
import jax
import jax.numpy as jnp
from jax import lax
from jax.sharding import PartitionSpec as P

ITERS = 2
EPSILON = 0.2
NEGATIVE = -1e30


def passed_along(array, axis, by):
    count = lax.axis_size(axis)
    return lax.ppermute(array, axis, [(i, (i + by) % count) for i in range(count)])


def combined_all(part, axis, combine):
    gathered = jax.tree.map(lambda a: lax.all_gather(a, axis), part)

    def take(source):
        return jax.tree.map(lambda a: lax.dynamic_index_in_dim(a, source, 0, False), gathered)

    return lax.fori_loop(
        1, lax.axis_size(axis), lambda source, state: combine(state, take(source)), take(0)
    )


def join_parts(first, second):
    highest = jnp.maximum(first[0], second[0])
    return (
        highest,
        first[1] * jnp.exp(first[0] - highest) + second[1] * jnp.exp(second[0] - highest),
    )


def lookup(cell_ids, slot_table):
    matches = cell_ids[:, None] == jnp.arange(slot_table.shape[0], dtype=jnp.int32)[None, :]
    return jnp.sum(jnp.where(matches, slot_table[None, :], 0), axis=1)


def half_norms(points, group_size, cell_rows):
    return 0.5 * jnp.sum(jnp.square(points.astype(jnp.float32)), axis=1).reshape(
        group_size, cell_rows
    )


def shards(tiles, cell_slot, counts, src_points, tgt_points):
    group_size = lax.axis_size("help")
    help_index = lax.axis_index("help")
    src_index = lax.axis_index("src")
    cell_rows = src_points.shape[0]
    width = src_points.shape[1]
    cost_scale = math.sqrt(width)
    source_all, source_counts = (src_points, counts)
    source_cells_held = 1
    own_points, own_counts = (
        lax.all_gather(tgt_points, "help", axis=0, tiled=True),
        lax.all_gather(counts, "help", axis=0, tiled=True),
    )
    next_points, next_counts = passed_along((own_points, own_counts), "src", -1)
    candidates = 2 * group_size
    positions = jnp.arange(cell_rows, dtype=jnp.int32)
    source_live = positions[None, :] < source_counts[:, 0:1]
    target_live = jnp.stack(
        [positions[None, :] < own_counts[:, 1:2], positions[None, :] < next_counts[:, 1:2]], axis=0
    )
    flat_live = target_live.reshape(candidates, cell_rows)
    source_half = half_norms(source_all, source_cells_held, cell_rows)
    target_half = jnp.stack(
        [
            half_norms(own_points, group_size, cell_rows),
            half_norms(next_points, group_size, cell_rows),
        ],
        axis=0,
    )
    flat_half = target_half.reshape(candidates, cell_rows)
    target_points = jnp.concatenate([own_points, next_points], axis=0)
    src_slot = lookup(tiles[0], cell_slot[0])
    tgt_slot = lookup(tiles[1], cell_slot[1])
    src_cells = src_slot % group_size
    tgt_cells = tgt_slot % group_size
    tgt_sides = jnp.where(tgt_slot // group_size == src_index, 0, 1)
    tgt_keys = tgt_sides * group_size + tgt_cells
    key_ids = jnp.arange(candidates, dtype=jnp.int32)
    is_mine = src_cells == help_index
    listed_keys = jnp.any(is_mine[:, None] & (tgt_keys[:, None] == key_ids[None, :]), axis=0)
    inner = lax.dot_general(
        src_points, target_points, (((1,), (1,)), ((), ())), preferred_element_type=jnp.float32
    )
    cost = (source_half[0][:, None] + flat_half.reshape(-1)[None, :] - inner) / cost_scale
    column_live = (flat_live & listed_keys[:, None]).reshape(-1)
    mask = source_live[0][:, None] & column_live[None, :]
    own_live = source_live[0]
    target_table = jnp.zeros((2, group_size, cell_rows), jnp.float32)
    source_table = jnp.zeros((source_cells_held, cell_rows), jnp.float32)
    source_own = jnp.zeros((cell_rows,), jnp.float32)
    target_own = jnp.zeros((cell_rows,), jnp.float32)
    for sweep in range(ITERS):
        row_flat_target = target_table.reshape(candidates, cell_rows)
        row_scores = jnp.where(
            mask, (row_flat_target.reshape(-1)[None, :] - cost) / EPSILON, NEGATIVE
        )
        part_max = jnp.max(row_scores, axis=1)
        part_sum = jnp.sum(jnp.exp(row_scores - part_max[:, None]), axis=1)
        row_source_own = jnp.where(own_live, -EPSILON * (part_max + jnp.log(part_sum)), 0.0)
        row_source_table = row_source_own[None, :]
        source_table = row_source_table
        source_own = row_source_own
        scores = jnp.where(mask, (source_table[0][:, None] - cost) / EPSILON, NEGATIVE)
        peaks = jnp.max(scores, axis=0)
        sums = jnp.sum(jnp.exp(scores - peaks[None, :]), axis=0)
        peaks = peaks.reshape(2, group_size, cell_rows)
        sums = sums.reshape(2, group_size, cell_rows)
        peaks, sums = combined_all((peaks, sums), "help", join_parts)
        carried_max, carried_sum = passed_along((peaks[1], sums[1]), "src", 1)
        joined = join_parts((peaks[0], sums[0]), (carried_max, carried_sum))
        target_group = jnp.where(target_live[0], -EPSILON * (joined[0] + jnp.log(joined[1])), 0.0)
        target_after = passed_along(target_group, "src", -1)
        col_target_table = jnp.stack([target_group, target_after], axis=0)
        col_target_own = target_group[help_index]
        target_table = col_target_table
        target_own = col_target_own
    flat_target = target_table.reshape(candidates, cell_rows)
    exponent = (source_table[0][:, None] + flat_target.reshape(-1)[None, :] - cost) / EPSILON
    weight = jnp.where(mask, jnp.exp(exponent), 0.0).astype(jnp.bfloat16)
    own_numerator = jnp.dot(weight, target_points, preferred_element_type=jnp.float32)
    own_denominator = jnp.sum(weight.astype(jnp.float32), axis=1)
    safe_total = jnp.where(own_live, own_denominator, 1.0)
    transport = jnp.where(own_live[:, None], own_numerator / safe_total[:, None], 0.0)
    return (source_own, target_own, transport)


def solution(mesh):
    in_specs = (
        P(None, "src"),
        P(),
        P(("src", "help"), None),
        P(("src", "help"), None),
        P(("src", "help"), None),
    )
    out_specs = (P(("src", "help")), P(("src", "help")), P(("src", "help"), None))
    return jax.shard_map(shards, mesh=mesh, in_specs=in_specs, out_specs=out_specs, check_vma=False)
```

profile of v0, /device:TPU:1, one launch (start us, length us, event | category | flops | bytes accessed | tf_op | source)
XLA Modules:
  0.0 362.8 jit_solution(11354192799630096327)
XLA Ops:
  7.9 75.9 %all-gather.3.cloned.1.call-done = bf16[4096,512]{1,0:T(8,128)(2,1)} async-done(((bf16[512,512]{1,0:T(8,128)(2,1)}), bf16[4096,512]{1,0:T(8,128)(2,1)}) %all-gather.3.cloned.1.call-update) | async-done | bytes 4194320 | tf_op jit(solution)/shard_map/all_gather | solution.py:57
  85.7 14.5 %all-gather = s32[8,1,2]{2,1,0:T(1,128)S(1)} all-gather(s32[1,1,2]{2,1,0:T(1,128)} %bitcast.156), channel_id=1, replica_groups=mesh['src'=4,'help'=8] {'help'}, dimensions={0}, use_global_device_ids=true | all-gather | bytes 72 | tf_op jit(solution)/shard_map/all_gather | solution.py:58
  100.3 4.6 %collective-permute-start = (s32[8,2]{0,1:T(2,128)S(1)}, s32[8,2]{0,1:T(2,128)S(1)}, u32[]{:S(2)}, u32[]{:S(2)}) collective-permute-start(s32[8,2]{0,1:T(2,128)S(1)} %bitcast.162), channel_id=1, source_target_pairs={{0,24},{8,0},{16,8},{24,16},{1,25},{9,1},{17,9},{25,17},{2,26},{10... | collective-permute-start | bytes 200 | tf_op jit(solution)/shard_map/ppermute | solution.py:14
  108.7 24.6 %collective-permute-done = s32[8,2]{0,1:T(2,128)S(1)} collective-permute-done((s32[8,2]{0,1:T(2,128)S(1)}, s32[8,2]{0,1:T(2,128)S(1)}, u32[]{:S(2)}, u32[]{:S(2)}) %collective-permute-start) | collective-permute-done | bytes 96 | tf_op jit(solution)/shard_map/ppermute | solution.py:14
  133.4 3.1 multiply_reduce_fusion.1
  136.5 4.4 %constant_dynamic-update-slice_fusion.1 = bf16[8192,512]{1,0:T(8,128)(2,1)} fusion(bf16[4096,512]{1,0:T(8,128)(2,1)} %all-gather.3.cloned.1.call-done), kind=kLoop, calls=%fused_computation.82 | loop fusion | bytes 8388608
  140.9 3.1 multiply_reduce_fusion
  144.0 4.4 %constant_dynamic-update-slice_fusion = bf16[8192,512]{1,0:T(8,128)(2,1)} fusion(bf16[8192,512]{1,0:T(8,128)(2,1)} %constant_dynamic-update-slice_fusion.1, bf16[4096,512]{1,0:T(8,128)(2,1)} %collective-permute-done.1), kind=kLoop, calls=%fused_computation.81 | loop fusion | bytes 8388608 | tf_op jit(solution)/shard_map/concatenate | solution.py:77
  148.4 10.4 %fusion.6 = (f32[512]{0:T(512)S(1)}, f32[512,8192]{0,1:T(8,128)S(1)}) fusion(pred[512]{0:T(512)(128)(4,1)S(1)} %iota_compare_fusion.6, pred[8192]{0:T(1024)(128)(4,1)S(1)} %and.81, bf16[8192,512]{1,0:T(8,128)(2,1)} %constant_dynamic-update-slice_fusion, bf16[512,512]{1,0:T(8,128)(2,1)S(1)} %copy-done.2, f32[8192]{0:T(1024)S(1)} %bitcast.153, ...), kind=kOutput, calls=%fused_computation.23 | convolution fusion | flops 4328521216 | bytes 25735680 | tf_op jit(solution)/shard_map/dot_general | solution.py:87
  158.9 7.0 %exponential_reduce_fusion.3 = f32[512]{0:T(512)S(1)} fusion(f32[512,8192]{0,1:T(8,128)S(1)} %get-tuple-element.304, f32[512]{0:T(512)S(1)} %get-tuple-element.303, pred[512]{0:T(512)(128)(4,1)S(1)} %iota_compare_fusion.6, pred[8192]{0:T(1024)(128)(4,1)S(1)} %and.81), kind=kLoop, calls=%fused_computation.22 | loop fusion | flops 25165312 | bytes 16790016 | tf_op jit(solution)/shard_map/reduce_sum | solution.py:104
  166.0 4.8 %fusion.7 = f32[8192]{0:T(1024)S(1)} fusion(f32[512,8192]{0,1:T(8,128)S(1)} %get-tuple-element.304, f32[512]{0:T(512)S(1)} %multiply_select_fusion.1, pred[512]{0:T(512)(128)(4,1)S(1)} %iota_compare_fusion.6, pred[8192]{0:T(1024)(128)(4,1)S(1)} %and.81), kind=kLoop, calls=%fused_computation.24 | loop fusion | flops 20963328 | bytes 16820736 | tf_op jit(solution)/shard_map/reduce_max | solution.py:110
  170.8 6.7 %exponential_reduce_fusion.2 = f32[8192]{0:T(1024)S(1)} fusion(f32[512,8192]{0,1:T(8,128)S(1)} %get-tuple-element.304, f32[8192]{0:T(1024)S(1)} %fusion.7, f32[512]{0:T(512)S(1)} %multiply_select_fusion.1, pred[512]{0:T(512)(128)(4,1)S(1)} %iota_compare_fusion.6, pred[8192]{0:T(1024)(128)(4,1)S(1)} %and.81), kind=kLoop, calls=%fused_computation.21 | loop fusion | flops 25157632 | bytes 16853504 | tf_op jit(solution)/shard_map/reduce_sum | solution.py:111
  177.5 24.8 %all_gather.21 = f32[8,2,8,512]{3,2,1,0:T(8,128)S(1)} all-gather(f32[1,2,8,512]{3,2,1,0:T(8,128)S(1)} %all_gather_reshape.13), channel_id=1, replica_groups=mesh['src'=4,'help'=8] {'help'}, dimensions={0}, use_global_device_ids=true | all-gather | bytes 294912 | tf_op jit(solution)/shard_map/all_gather | solution.py:18
  202.4 24.9 %all_gather.20 = f32[8,2,8,512]{3,2,1,0:T(8,128)S(1)} all-gather(f32[1,2,8,512]{3,2,1,0:T(8,128)S(1)} %all_gather_reshape.12), channel_id=1, replica_groups=mesh['src'=4,'help'=8] {'help'}, dimensions={0}, use_global_device_ids=true | all-gather | bytes 294912 | tf_op jit(solution)/shard_map/all_gather | solution.py:18
  227.7 11.7 %collective-permute-start.2 = (f32[8,512]{1,0:T(8,128)S(1)}, f32[8,512]{1,0:T(8,128)S(1)}, u32[]{:S(2)}, u32[]{:S(2)}) collective-permute-start(f32[8,512]{1,0:T(8,128)S(1)} %slice_bitcast_fusion.7), channel_id=1, source_target_pairs={{0,8},{8,16},{16,24},{24,0},{1,9},{9,17},{17,25},{25,1},{2,10},{10... | collective-permute-start | bytes 49160 | tf_op jit(solution)/shard_map/ppermute | solution.py:14
  244.3 10.3 %fusion.8 = f32[512]{0:T(512)S(1)} fusion(f32[512,8192]{0,1:T(8,128)} %copy-done, f32[8192]{0:T(1024)S(1)} %bitcast.146, pred[512]{0:T(512)(128)(4,1)S(1)} %iota_compare_fusion.6, pred[8192]{0:T(1024)(128)(4,1)S(1)} %and.81), kind=kLoop, calls=%fused_computation.25 | loop fusion | flops 20971008 | bytes 16820736 | tf_op jit(solution)/shard_map/reduce_max | solution.py:103
  254.6 5.6 %exponential_reduce_fusion.1 = f32[512]{0:T(512)S(1)} fusion(f32[512,8192]{0,1:T(8,128)S(1)} %copy-done.1, f32[512]{0:T(512)S(1)} %fusion.8, f32[8192]{0:T(1024)S(1)} %bitcast.147, pred[512]{0:T(512)(128)(4,1)S(1)} %iota_compare_fusion.6, pred[8192]{0:T(1024)(128)(4,1)S(1)} %and.81), kind=kLoop, calls=%fused_computation.20 | loop fusion | flops 25165312 | bytes 16822784 | tf_op jit(solution)/shard_map/reduce_sum | solution.py:104
  260.2 4.8 %fusion.9 = f32[8192]{0:T(1024)S(1)} fusion(f32[512,8192]{0,1:T(8,128)S(1)} %copy-done.1, f32[512]{0:T(512)S(1)} %multiply_select_fusion, pred[512]{0:T(512)(128)(4,1)S(1)} %iota_compare_fusion.6, pred[8192]{0:T(1024)(128)(4,1)S(1)} %and.81), kind=kLoop, calls=%fused_computation.26 | loop fusion | flops 20963328 | bytes 16820736 | tf_op jit(solution)/shard_map/reduce_max | solution.py:110
  265.1 6.7 %exponential_reduce_fusion = f32[8192]{0:T(1024)S(1)} fusion(f32[512,8192]{0,1:T(8,128)S(1)} %copy-done.1, f32[8192]{0:T(1024)S(1)} %fusion.9, f32[512]{0:T(512)S(1)} %multiply_select_fusion, pred[512]{0:T(512)(128)(4,1)S(1)} %iota_compare_fusion.6, pred[8192]{0:T(1024)(128)(4,1)S(1)} %and.81), kind=kLoop, calls=%fused_computation.19 | loop fusion | flops 25157632 | bytes 16853504 | tf_op jit(solution)/shard_map/reduce_sum | solution.py:111
  271.8 25.1 %all_gather.23 = f32[8,2,8,512]{3,2,1,0:T(8,128)S(1)} all-gather(f32[1,2,8,512]{3,2,1,0:T(8,128)S(1)} %all_gather_reshape.15), channel_id=1, replica_groups=mesh['src'=4,'help'=8] {'help'}, dimensions={0}, use_global_device_ids=true | all-gather | bytes 294912 | tf_op jit(solution)/shard_map/all_gather | solution.py:18
  296.9 24.9 %all_gather.22 = f32[8,2,8,512]{3,2,1,0:T(8,128)S(1)} all-gather(f32[1,2,8,512]{3,2,1,0:T(8,128)S(1)} %all_gather_reshape.14), channel_id=1, replica_groups=mesh['src'=4,'help'=8] {'help'}, dimensions={0}, use_global_device_ids=true | all-gather | bytes 294912 | tf_op jit(solution)/shard_map/all_gather | solution.py:18
  322.2 11.8 %collective-permute-start.5 = (f32[8,512]{1,0:T(8,128)S(1)}, f32[8,512]{1,0:T(8,128)S(1)}, u32[]{:S(2)}, u32[]{:S(2)}) collective-permute-start(f32[8,512]{1,0:T(8,128)S(1)} %slice_bitcast_fusion.5), channel_id=1, source_target_pairs={{0,8},{8,16},{16,24},{24,0},{1,9},{9,17},{17,25},{25,1},{2,10},{10... | collective-permute-start | bytes 49160 | tf_op jit(solution)/shard_map/ppermute | solution.py:14
  338.9 8.1 %convert_reduce_fusion = (f32[512]{0:T(512)S(1)}, bf16[512,8192]{0,1:T(8,128)(2,1)S(1)}) fusion(f32[512,8192]{0,1:T(8,128)} %copy-done, f32[8192]{0:T(1024)S(1)} %bitcast.148, f32[512]{0:T(512)S(1)} %multiply_select_fusion, pred[8192]{0:T(1024)(128)(4,1)S(1)} %and.81, pred[512]{0:T(512)(128)(4,1)S(1)} %iota_compare_fusion.6), kind=kLoop, calls=%fused_computation.18 | loop fusion | flops 33553920 | bytes 25211392 | tf_op jit(solution)/shard_map/reduce_sum | solution.py:127
  347.1 8.9 %fusion.10 = f32[512,512]{1,0:T(8,128)} fusion(bf16[512,8192]{0,1:T(8,128)(2,1)S(1)} %get-tuple-element.298, bf16[8192,512]{1,0:T(8,128)(2,1)} %constant_dynamic-update-slice_fusion, f32[512]{0:T(512)S(1)} %broadcast_select_fusion, pred[512]{0:T(512)(128)(4,1)S(1)} %iota_compare_fusion.6), kind=kOutput, calls=%fused_computation.30 | convolution fusion | flops 4295491584 | bytes 17828352 | tf_op jit(solution)/shard_map/dot_general | solution.py:126
  (87 shorter events, 17.8 us)
Async XLA Ops:
  7.2 141.3 %copy-start.2 = (bf16[512,512]{1,0:T(8,128)(2,1)S(1)}, bf16[512,512]{1,0:T(8,128)(2,1)}, u32[]{:S(2)}) copy-start(bf16[512,512]{1,0:T(8,128)(2,1)} %param.12) | copy-start | bytes 1572868
  7.2 76.6 %all-gather.3.cloned.1.call-start = ((), (), s32[]{:S(2)}) async-start(), calls=%async_computation | async-start | bytes 4718592 | tf_op jit(solution)/shard_map/all_gather | solution.py:57
  83.8 57.1 %collective-permute-start.1 = (bf16[4096,512]{1,0:T(8,128)(2,1)}, bf16[4096,512]{1,0:T(8,128)(2,1)}, u32[]{:S(2)}, u32[]{:S(2)}) collective-permute-start(bf16[4096,512]{1,0:T(8,128)(2,1)} %all-gather.3.cloned.1.call-done), channel_id=1, source_target_pairs={{0,24},{8,0},{16,8},{24,16},{1,25},{9,1},{17,9},{25,17},{2,26},{10... | collective-permute-start | bytes 12582920 | tf_op jit(solution)/shard_map/ppermute | solution.py:14
  100.3 33.0 %collective-permute-start = (s32[8,2]{0,1:T(2,128)S(1)}, s32[8,2]{0,1:T(2,128)S(1)}, u32[]{:S(2)}, u32[]{:S(2)}) collective-permute-start(s32[8,2]{0,1:T(2,128)S(1)} %bitcast.162), channel_id=1, source_target_pairs={{0,24},{8,0},{16,8},{24,16},{1,25},{9,1},{17,9},{25,17},{2,26},{10... | collective-permute-start | bytes 200 | tf_op jit(solution)/shard_map/ppermute | solution.py:14
  158.9 11.9 %copy-start = (f32[512,8192]{0,1:T(8,128)}, f32[512,8192]{0,1:T(8,128)S(1)}, u32[]{:S(2)}) copy-start(f32[512,8192]{0,1:T(8,128)S(1)} %get-tuple-element.304) | copy-start | bytes 50331652
  158.9 7.0 %copy-start.4 = (s32[1,2]{1,0:T(1,128)S(1)}, s32[1,2]{1,0:T(1,128)}, u32[]{:S(2)}) copy-start(s32[1,2]{1,0:T(1,128)} %param.11) | copy-start | bytes 28
  227.7 12.6 %collective-permute-start.2 = (f32[8,512]{1,0:T(8,128)S(1)}, f32[8,512]{1,0:T(8,128)S(1)}, u32[]{:S(2)}, u32[]{:S(2)}) collective-permute-start(f32[8,512]{1,0:T(8,128)S(1)} %slice_bitcast_fusion.7), channel_id=1, source_target_pairs={{0,8},{8,16},{16,24},{24,0},{1,9},{9,17},{17,25},{25,1},{2,10},{10... | collective-permute-start | bytes 49160 | tf_op jit(solution)/shard_map/ppermute | solution.py:14
  239.4 1.2 collective-permute-start.3
  240.7 3.6 collective-permute-start.4
  242.0 12.6 %copy-start.1 = (f32[512,8192]{0,1:T(8,128)S(1)}, f32[512,8192]{0,1:T(8,128)}, u32[]{:S(2)}) copy-start(f32[512,8192]{0,1:T(8,128)} %copy-done) | copy-start | bytes 50331652
  260.2 78.7 %copy-start.3 = (f32[512]{0:T(512)}, f32[512]{0:T(512)S(1)}, u32[]{:S(2)}) copy-start(f32[512]{0:T(512)S(1)} %multiply_select_fusion) | copy-start | bytes 6148
  322.2 12.7 %collective-permute-start.5 = (f32[8,512]{1,0:T(8,128)S(1)}, f32[8,512]{1,0:T(8,128)S(1)}, u32[]{:S(2)}, u32[]{:S(2)}) collective-permute-start(f32[8,512]{1,0:T(8,128)S(1)} %slice_bitcast_fusion.5), channel_id=1, source_target_pairs={{0,8},{8,16},{16,24},{24,0},{1,9},{9,17},{17,25},{25,1},{2,10},{10... | collective-permute-start | bytes 49160 | tf_op jit(solution)/shard_map/ppermute | solution.py:14
  334.1 1.2 collective-permute-start.6
  335.3 3.6 collective-permute-start.7
Sparse Core Ops, SparseCore 0:
  10.1 73.6 all-gather.2
where the time goes:
time: 363 us
  blocking collectives  114 us (31%)
  waiting for transfers between devices  107 us (29%)
  other arithmetic  63.1 us (17%)
  starting transfers between devices  32.9 us (9%)
  matrix products  19.3 us (5%)
  between operations  14.4 us (4%)
  local copies, waits for them, and re-layouts  11.2 us (3%)
    all_gather x4, blocking collectives, combined_all(): gathered = jax.tree.map(lambda a: lax.all_gather(a, axis), part)  99.8 us
    all_gather x1, waiting for transfers between devices, shards(): lax.all_gather(tgt_points, 'help', axis=0, tiled=True)  75.9 us
    ppermute x8, starting transfers between devices, passed_along(): lax.ppermute(array, axis, [(i, (i + by) % count) for i in range(count)])  32.8 us
    ppermute x8, waiting for transfers between devices, passed_along(): lax.ppermute(array, axis, [(i, (i + by) % count) for i in range(count)])  30.7 us
    all_gather x1, blocking collectives, shards(): lax.all_gather(counts, 'help', axis=0, tiled=True)  14.5 us
    reduce_sum x2, other arithmetic, shards(): sums = jnp.sum(jnp.exp(scores - peaks[None, :]), axis=0)  13.3 us
    reduce_sum x2, other arithmetic, shards(): part_sum = jnp.sum(jnp.exp(row_scores - part_max[:, None]), axis=1)  12.6 us
    dot_general x1, matrix products, shards(): lax.dot_general(src_points, target_points, (((1,), (1,)), ((), ())), pref...  10.4 us
  transfers between devices with their start and end apart: 9, of which 8 were waited for; matrix products, arithmetic and copies ran while one was open for 3% of the time, Pallas kernels for 0%

commit v1 on v0

--- a/solution.py
+++ b/solution.py
@@ -7,6 +7,18 @@
 ITERS = 2
 EPSILON = 0.2
 NEGATIVE = -1e30
+
+
+def _lay_teams(xin, axis_tag="help"):
+    spare, all_rows, block_next = (lax.axis_size(axis_tag), lax.axis_index(axis_tag), xin.shape[0])
+    later, z2 = (xin, 1)
+    while z2 < spare:
+        later = jnp.concatenate(
+            [later, lax.ppermute(later, axis_tag, [(c, (c - z2) % spare) for c in range(spare)])], 0
+        )
+        z2 = 2 * z2
+    step_out = jnp.roll(later, all_rows * block_next, 0)
+    return step_out
 
 
 def passed_along(array, axis, by):
@@ -54,7 +66,7 @@
     source_all, source_counts = (src_points, counts)
     source_cells_held = 1
     own_points, own_counts = (
-        lax.all_gather(tgt_points, "help", axis=0, tiled=True),
+        _lay_teams(tgt_points),
         lax.all_gather(counts, "help", axis=0, tiled=True),
     )
     next_points, next_counts = passed_along((own_points, own_counts), "src", -1)

time: 363 us -> 404 us (1.11)
  waiting for transfers between devices: 107 us -> 152 us
  between operations: 14.4 us -> 1.1 us
  starting transfers between devices: 32.9 us -> 40.5 us
  local copies, waits for them, and re-layouts: 11.2 us -> 4.24 us
    ppermute x0 -> x3, waiting for transfers between devices: none -> 123 us  [_lay_teams(): lax.ppermute(later, axis_tag, [(c, (c - z2) % spare) for c in range(spare)])]
    all_gather x1 -> x0, waiting for transfers between devices: 75.9 us -> none  [shards(): lax.all_gather(tgt_points, 'help', axis=0, tiled=True)]
    ppermute x0 -> x3, starting transfers between devices: none -> 6.5 us  [_lay_teams(): lax.ppermute(later, axis_tag, [(c, (c - z2) % spare) for c in range(spare)])]
    concatenate x1, local copies, waits for them, and re-layouts: 4.43 us -> 0.14 us  [_lay_teams(): step_out = jnp.roll(later, all_rows * block_next, 0)]
  transfers between devices with their start and end apart: 9 -> 11, of which waited for: 8 -> 10; matrix products, arithmetic and copies ran while one was open for 3% -> 1% of each run, Pallas kernels for 0% -> 0%
where the time goes in v1:
time: 404 us; the launch traced here: 403 us
  waiting for transfers between devices  152 us (38%)
  blocking collectives  118 us (29%)
  other arithmetic  65.9 us (16%)
  starting transfers between devices  40.5 us (10%)
  matrix products  22.1 us (5%)
  local copies, waits for them, and re-layouts  4.24 us (1%)
    ppermute x3, waiting for transfers between devices, _lay_teams(): lax.ppermute(later, axis_tag, [(c, (c - z2) % spare) for c in range(spare)])  123 us
    all_gather x4, blocking collectives, combined_all(): gathered = jax.tree.map(lambda a: lax.all_gather(a, axis), part)  100 us
    ppermute x8, starting transfers between devices, passed_along(): lax.ppermute(array, axis, [(i, (i + by) % count) for i in range(count)])  34 us
    ppermute x8, waiting for transfers between devices, passed_along(): lax.ppermute(array, axis, [(i, (i + by) % count) for i in range(count)])  28.1 us
    all_gather x1, blocking collectives, shards(): lax.all_gather(counts, 'help', axis=0, tiled=True)  17.6 us
    reduce_sum x2, other arithmetic, shards(): sums = jnp.sum(jnp.exp(scores - peaks[None, :]), axis=0)  13.4 us
    dot_general x1, matrix products, shards(): lax.dot_general(src_points, target_points, (((1,), (1,)), ((), ())), pref...  13.1 us
    reduce_sum x2, other arithmetic, shards(): part_sum = jnp.sum(jnp.exp(row_scores - part_max[:, None]), axis=1)  12.6 us
  transfers between devices with their start and end apart: 11, of which 10 were waited for; matrix products, arithmetic and copies ran while one was open for 1% of the time, Pallas kernels for 0%

profile of v1, /device:TPU:1, one launch (start us, length us, event | category | flops | bytes accessed | tf_op | source)
XLA Modules:
  0.0 403.3 jit_solution(18038737033744215727)
XLA Ops:
  0.6 5.1 %collective-permute-start.1 = (bf16[512,512]{1,0:T(8,128)(2,1)}, bf16[512,512]{1,0:T(8,128)(2,1)S(1)}, u32[]{:S(2)}, u32[]{:S(2)}) collective-permute-start(bf16[512,512]{1,0:T(8,128)(2,1)} %param.13), channel_id=1, source_target_pairs={{0,7},{1,0},{2,1},{3,2},{4,3},{5,4},{6,5},{7,6},{8,15},{9,8},{10,9... | collective-permute-start | bytes 1572872 | tf_op jit(solution)/shard_map/ppermute | solution.py:17
  5.7 10.9 %collective-permute-done.1 = bf16[512,512]{1,0:T(8,128)(2,1)S(1)} collective-permute-done((bf16[512,512]{1,0:T(8,128)(2,1)}, bf16[512,512]{1,0:T(8,128)(2,1)S(1)}, u32[]{:S(2)}, u32[]{:S(2)}) %collective-permute-start.1) | collective-permute-done | bytes 524320 | tf_op jit(solution)/shard_map/ppermute | solution.py:17
  19.2 22.0 %collective-permute-done.2 = bf16[1024,512]{1,0:T(8,128)(2,1)S(1)} collective-permute-done((bf16[1024,512]{1,0:T(8,128)(2,1)S(1)}, bf16[1024,512]{1,0:T(8,128)(2,1)S(1)}, u32[]{:S(2)}, u32[]{:S(2)}) %collective-permute-start.2) | collective-permute-done | bytes 1048608 | tf_op jit(solution)/shard_map/ppermute | solution.py:17
  46.2 90.5 %collective-permute-done.3 = bf16[2048,512]{1,0:T(8,128)(2,1)S(1)} collective-permute-done((bf16[2048,512]{1,0:T(8,128)(2,1)}, bf16[2048,512]{1,0:T(8,128)(2,1)S(1)}, u32[]{:S(2)}, u32[]{:S(2)}) %collective-permute-start.3) | collective-permute-done | bytes 2097184 | tf_op jit(solution)/shard_map/ppermute | solution.py:17
  141.1 17.6 %all-gather = s32[8,1,2]{2,1,0:T(1,128)S(1)} all-gather(s32[1,1,2]{2,1,0:T(1,128)S(1)} %bitcast.154), channel_id=1, replica_groups=mesh['src'=4,'help'=8] {'help'}, dimensions={0}, use_global_device_ids=true | all-gather | bytes 72 | tf_op jit(solution)/shard_map/all_gather | solution.py:70
  158.8 4.9 %collective-permute-start = (s32[8,2]{0,1:T(2,128)S(1)}, s32[8,2]{0,1:T(2,128)S(1)}, u32[]{:S(2)}, u32[]{:S(2)}) collective-permute-start(s32[8,2]{0,1:T(2,128)S(1)} %bitcast.160), channel_id=1, source_target_pairs={{0,24},{8,0},{16,8},{24,16},{1,25},{9,1},{17,9},{25,17},{2,26},{10... | collective-permute-start | bytes 200 | tf_op jit(solution)/shard_map/ppermute | solution.py:26
  165.4 23.3 %collective-permute-done = s32[8,2]{0,1:T(2,128)S(1)} collective-permute-done((s32[8,2]{0,1:T(2,128)S(1)}, s32[8,2]{0,1:T(2,128)S(1)}, u32[]{:S(2)}, u32[]{:S(2)}) %collective-permute-start) | collective-permute-done | bytes 96 | tf_op jit(solution)/shard_map/ppermute | solution.py:26
  188.9 3.1 multiply_reduce_fusion
  192.0 13.1 %fusion.6 = (f32[512]{0:T(512)S(1)}, f32[512,8192]{0,1:T(8,128)S(1)}) fusion(pred[512]{0:T(512)(128)(4,1)S(1)} %iota_compare_fusion.6, pred[8192]{0:T(1024)(128)(4,1)S(1)} %and.87, bf16[512,512]{1,0:T(8,128)(2,1)S(1)} %copy-done.5, bf16[4096,512]{1,0:T(8,128)(2,1)} %collective-permute-done.4, bf16[4096,512]{1,0:T(8,128)(2,1)} %get-tuple-element.300, ...), kind=kOutput, calls=%fused_computation.23 | convolution fusion | flops 4345298432 | bytes 25735680 | tf_op jit(solution)/shard_map/dot_general | solution.py:99
  205.2 7.0 %exponential_reduce_fusion.3 = f32[512]{0:T(512)S(1)} fusion(f32[512,8192]{0,1:T(8,128)S(1)} %get-tuple-element.306, f32[512]{0:T(512)S(1)} %get-tuple-element.305, pred[512]{0:T(512)(128)(4,1)S(1)} %iota_compare_fusion.6, pred[8192]{0:T(1024)(128)(4,1)S(1)} %and.87), kind=kLoop, calls=%fused_computation.22 | loop fusion | flops 25165312 | bytes 16790016 | tf_op jit(solution)/shard_map/reduce_sum | solution.py:116
  212.3 4.8 %fusion.7 = f32[8192]{0:T(1024)S(1)} fusion(f32[512,8192]{0,1:T(8,128)S(1)} %get-tuple-element.306, f32[512]{0:T(512)S(1)} %multiply_select_fusion.1, pred[512]{0:T(512)(128)(4,1)S(1)} %iota_compare_fusion.6, pred[8192]{0:T(1024)(128)(4,1)S(1)} %and.87), kind=kLoop, calls=%fused_computation.24 | loop fusion | flops 20963328 | bytes 16820736 | tf_op jit(solution)/shard_map/reduce_max | solution.py:122
  217.1 6.7 %exponential_reduce_fusion.2 = f32[8192]{0:T(1024)S(1)} fusion(f32[512,8192]{0,1:T(8,128)S(1)} %get-tuple-element.306, f32[8192]{0:T(1024)S(1)} %fusion.7, f32[512]{0:T(512)S(1)} %multiply_select_fusion.1, pred[512]{0:T(512)(128)(4,1)S(1)} %iota_compare_fusion.6, pred[8192]{0:T(1024)(128)(4,1)S(1)} %and.87), kind=kLoop, calls=%fused_computation.21 | loop fusion | flops 25157632 | bytes 16853504 | tf_op jit(solution)/shard_map/reduce_sum | solution.py:123
  223.8 25.6 %all_gather.17 = f32[8,2,8,512]{3,2,1,0:T(8,128)S(1)} all-gather(f32[1,2,8,512]{3,2,1,0:T(8,128)S(1)} %all_gather_reshape.13), channel_id=1, replica_groups=mesh['src'=4,'help'=8] {'help'}, dimensions={0}, use_global_device_ids=true | all-gather | bytes 294912 | tf_op jit(solution)/shard_map/all_gather | solution.py:30
  249.5 24.6 %all_gather.16 = f32[8,2,8,512]{3,2,1,0:T(8,128)S(1)} all-gather(f32[1,2,8,512]{3,2,1,0:T(8,128)S(1)} %all_gather_reshape.12), channel_id=1, replica_groups=mesh['src'=4,'help'=8] {'help'}, dimensions={0}, use_global_device_ids=true | all-gather | bytes 294912 | tf_op jit(solution)/shard_map/all_gather | solution.py:30
  274.5 11.8 %collective-permute-start.5 = (f32[8,512]{1,0:T(8,128)S(1)}, f32[8,512]{1,0:T(8,128)S(1)}, u32[]{:S(2)}, u32[]{:S(2)}) collective-permute-start(f32[8,512]{1,0:T(8,128)S(1)} %slice_bitcast_fusion.7), channel_id=1, source_target_pairs={{0,8},{8,16},{16,24},{24,0},{1,9},{9,17},{17,25},{25,1},{2,10},{10... | collective-permute-start | bytes 49160 | tf_op jit(solution)/shard_map/ppermute | solution.py:26
  291.3 10.1 %fusion.8 = f32[512]{0:T(512)S(1)} fusion(f32[512,8192]{0,1:T(8,128)} %copy-done, f32[8192]{0:T(1024)S(1)} %bitcast.144, pred[512]{0:T(512)(128)(4,1)S(1)} %iota_compare_fusion.6, pred[8192]{0:T(1024)(128)(4,1)S(1)} %and.87), kind=kLoop, calls=%fused_computation.25 | loop fusion | flops 20971008 | bytes 16820736 | tf_op jit(solution)/shard_map/reduce_max | solution.py:115
  302.0 5.6 %exponential_reduce_fusion.1 = f32[512]{0:T(512)S(1)} fusion(f32[512,8192]{0,1:T(8,128)S(1)} %copy-done.1, f32[512]{0:T(512)S(1)} %fusion.8, f32[8192]{0:T(1024)S(1)} %bitcast.145, pred[512]{0:T(512)(128)(4,1)S(1)} %iota_compare_fusion.6, pred[8192]{0:T(1024)(128)(4,1)S(1)} %and.87), kind=kLoop, calls=%fused_computation.20 | loop fusion | flops 25165312 | bytes 16822784 | tf_op jit(solution)/shard_map/reduce_sum | solution.py:116
  307.7 4.8 %fusion.9 = f32[8192]{0:T(1024)S(1)} fusion(f32[512,8192]{0,1:T(8,128)S(1)} %copy-done.1, f32[512]{0:T(512)S(1)} %multiply_select_fusion, pred[512]{0:T(512)(128)(4,1)S(1)} %iota_compare_fusion.6, pred[8192]{0:T(1024)(128)(4,1)S(1)} %and.87), kind=kLoop, calls=%fused_computation.26 | loop fusion | flops 20963328 | bytes 16820736 | tf_op jit(solution)/shard_map/reduce_max | solution.py:122
  312.5 6.7 %exponential_reduce_fusion = f32[8192]{0:T(1024)S(1)} fusion(f32[512,8192]{0,1:T(8,128)S(1)} %copy-done.1, f32[8192]{0:T(1024)S(1)} %fusion.9, f32[512]{0:T(512)S(1)} %multiply_select_fusion, pred[512]{0:T(512)(128)(4,1)S(1)} %iota_compare_fusion.6, pred[8192]{0:T(1024)(128)(4,1)S(1)} %and.87), kind=kLoop, calls=%fused_computation.19 | loop fusion | flops 25157632 | bytes 16853504 | tf_op jit(solution)/shard_map/reduce_sum | solution.py:123
  319.2 25.1 %all_gather.19 = f32[8,2,8,512]{3,2,1,0:T(8,128)S(1)} all-gather(f32[1,2,8,512]{3,2,1,0:T(8,128)S(1)} %all_gather_reshape.15), channel_id=1, replica_groups=mesh['src'=4,'help'=8] {'help'}, dimensions={0}, use_global_device_ids=true | all-gather | bytes 294912 | tf_op jit(solution)/shard_map/all_gather | solution.py:30
  344.4 24.7 %all_gather.18 = f32[8,2,8,512]{3,2,1,0:T(8,128)S(1)} all-gather(f32[1,2,8,512]{3,2,1,0:T(8,128)S(1)} %all_gather_reshape.14), channel_id=1, replica_groups=mesh['src'=4,'help'=8] {'help'}, dimensions={0}, use_global_device_ids=true | all-gather | bytes 294912 | tf_op jit(solution)/shard_map/all_gather | solution.py:30
  369.5 11.8 %collective-permute-start.8 = (f32[8,512]{1,0:T(8,128)S(1)}, f32[8,512]{1,0:T(8,128)S(1)}, u32[]{:S(2)}, u32[]{:S(2)}) collective-permute-start(f32[8,512]{1,0:T(8,128)S(1)} %slice_bitcast_fusion.5), channel_id=1, source_target_pairs={{0,8},{8,16},{16,24},{24,0},{1,9},{9,17},{17,25},{25,1},{2,10},{10... | collective-permute-start | bytes 49160 | tf_op jit(solution)/shard_map/ppermute | solution.py:26
  386.2 8.1 %convert_reduce_fusion = (f32[512]{0:T(512)S(1)}, bf16[512,8192]{0,1:T(8,128)(2,1)S(1)}) fusion(f32[512,8192]{0,1:T(8,128)} %copy-done, f32[8192]{0:T(1024)S(1)} %bitcast.146, f32[512]{0:T(512)S(1)} %multiply_select_fusion, pred[8192]{0:T(1024)(128)(4,1)S(1)} %and.87, pred[512]{0:T(512)(128)(4,1)S(1)} %iota_compare_fusion.6), kind=kLoop, calls=%fused_computation.18 | loop fusion | flops 33553920 | bytes 25211392 | tf_op jit(solution)/shard_map/reduce_sum | solution.py:139
  394.3 9.0 %fusion.12 = f32[512,512]{1,0:T(8,128)} fusion(bf16[512,8192]{0,1:T(8,128)(2,1)S(1)} %get-tuple-element.298, bf16[4096,512]{1,0:T(8,128)(2,1)} %collective-permute-done.4, bf16[4096,512]{1,0:T(8,128)(2,1)} %get-tuple-element.300, f32[512]{0:T(512)S(1)} %broadcast_select_fusion, pred[512]{0:T(512)(128)(4,1)S(1)} %iota_compare_fusion.6), kind=kOutput, calls=%fused_computation.33 | convolution fusion | flops 4312268800 | bytes 17828352 | tf_op jit(solution)/shard_map/dot_general | solution.py:138
  (108 shorter events, 25.6 us)
Async XLA Ops:
  0.6 16.0 %collective-permute-start.1 = (bf16[512,512]{1,0:T(8,128)(2,1)}, bf16[512,512]{1,0:T(8,128)(2,1)S(1)}, u32[]{:S(2)}, u32[]{:S(2)}) collective-permute-start(bf16[512,512]{1,0:T(8,128)(2,1)} %param.13), channel_id=1, source_target_pairs={{0,7},{1,0},{2,1},{3,2},{4,3},{5,4},{6,5},{7,6},{8,15},{9,8},{10,9... | collective-permute-start | bytes 1572872 | tf_op jit(solution)/shard_map/ppermute | solution.py:17
  16.7 24.5 %copy-start.3 = (bf16[512,512]{1,0:T(8,128)(2,1)}, bf16[512,512]{1,0:T(8,128)(2,1)S(1)}, u32[]{:S(2)}) copy-start(bf16[512,512]{1,0:T(8,128)(2,1)S(1)} %collective-permute-done.1) | copy-start | bytes 1572868
  18.0 23.2 %collective-permute-start.2 = (bf16[1024,512]{1,0:T(8,128)(2,1)S(1)}, bf16[1024,512]{1,0:T(8,128)(2,1)S(1)}, u32[]{:S(2)}, u32[]{:S(2)}) collective-permute-start(bf16[1024,512]{1,0:T(8,128)(2,1)S(1)} %pad_maximum_fusion.8), channel_id=1, source_target_pairs={{0,6},{1,7},{2,0},{3,1},{4,2},{5,3},{6,4},{7,5},{8,14},{9,15},{10,... | collective-permute-start | bytes 3145736 | tf_op jit(solution)/shard_map/ppermute | solution.py:17
  43.7 93.0 %collective-permute-start.3 = (bf16[2048,512]{1,0:T(8,128)(2,1)}, bf16[2048,512]{1,0:T(8,128)(2,1)S(1)}, u32[]{:S(2)}, u32[]{:S(2)}) collective-permute-start(bf16[2048,512]{1,0:T(8,128)(2,1)} %pad_maximum_fusion.3), channel_id=1, source_target_pairs={{0,4},{1,5},{2,6},{3,7},{4,0},{5,1},{6,2},{7,3},{8,12},{9,13},{10,... | collective-permute-start | bytes 6291464 | tf_op jit(solution)/shard_map/ppermute | solution.py:17
  43.9 93.0 %copy-start.2 = (bf16[512,512]{1,0:T(8,128)(2,1)S(1)}, bf16[512,512]{1,0:T(8,128)(2,1)}, u32[]{:S(2)}) copy-start(bf16[512,512]{1,0:T(8,128)(2,1)} %param.13) | copy-start | bytes 1572868
  43.9 93.1 %copy-start.4 = (bf16[512,512]{1,0:T(8,128)(2,1)S(1)}, bf16[512,512]{1,0:T(8,128)(2,1)}, u32[]{:S(2)}) copy-start(bf16[512,512]{1,0:T(8,128)(2,1)} %copy-done.3) | copy-start | bytes 1572868
  136.9 4.2 %copy-start.7 = (s32[1,2]{1,0:T(1,128)S(1)}, s32[1,2]{1,0:T(1,128)}, u32[]{:S(2)}) copy-start(s32[1,2]{1,0:T(1,128)} %param.11) | copy-start | bytes 28
  136.9 26.8 %copy-start.8 = (s32[2,64]{1,0:T(2,128)S(1)}, s32[2,64]{1,0:T(2,128)}, u32[]{:S(2)}) copy-start(s32[2,64]{1,0:T(2,128)} %param.9) | copy-start | bytes 1540
  136.9 26.8 %copy-start.9 = (s32[2,32]{1,0:T(2,128)S(1)}, s32[2,32]{1,0:T(2,128)}, u32[]{:S(2)}) copy-start(s32[2,32]{1,0:T(2,128)} %param.10) | copy-start | bytes 772
  137.1 54.9 %copy-start.5 = (bf16[512,512]{1,0:T(8,128)(2,1)S(1)}, bf16[512,512]{1,0:T(8,128)(2,1)}, u32[]{:S(2)}) copy-start(bf16[512,512]{1,0:T(8,128)(2,1)} %param.12) | copy-start | bytes 1572868
  140.0 48.9 %collective-permute-start.4 = (bf16[4096,512]{1,0:T(8,128)(2,1)}, bf16[4096,512]{1,0:T(8,128)(2,1)}, u32[]{:S(2)}, u32[]{:S(2)}) collective-permute-start(bf16[4096,512]{1,0:T(8,128)(2,1)} %get-tuple-element.300), channel_id=1, source_target_pairs={{0,24},{8,0},{16,8},{24,16},{1,25},{9,1},{17,9},{25,17},{2,26},{10... | collective-permute-start | bytes 12582920 | tf_op jit(solution)/shard_map/ppermute | solution.py:26
  158.8 30.0 %collective-permute-start = (s32[8,2]{0,1:T(2,128)S(1)}, s32[8,2]{0,1:T(2,128)S(1)}, u32[]{:S(2)}, u32[]{:S(2)}) collective-permute-start(s32[8,2]{0,1:T(2,128)S(1)} %bitcast.160), channel_id=1, source_target_pairs={{0,24},{8,0},{16,8},{24,16},{1,25},{9,1},{17,9},{25,17},{2,26},{10... | collective-permute-start | bytes 200 | tf_op jit(solution)/shard_map/ppermute | solution.py:26
  205.2 11.9 %copy-start = (f32[512,8192]{0,1:T(8,128)}, f32[512,8192]{0,1:T(8,128)S(1)}, u32[]{:S(2)}) copy-start(f32[512,8192]{0,1:T(8,128)S(1)} %get-tuple-element.306) | copy-start | bytes 50331652
  274.5 12.7 %collective-permute-start.5 = (f32[8,512]{1,0:T(8,128)S(1)}, f32[8,512]{1,0:T(8,128)S(1)}, u32[]{:S(2)}, u32[]{:S(2)}) collective-permute-start(f32[8,512]{1,0:T(8,128)S(1)} %slice_bitcast_fusion.7), channel_id=1, source_target_pairs={{0,8},{8,16},{16,24},{24,0},{1,9},{9,17},{17,25},{25,1},{2,10},{10... | collective-permute-start | bytes 49160 | tf_op jit(solution)/shard_map/ppermute | solution.py:26
  286.3 1.2 collective-permute-start.6
  287.5 3.8 collective-permute-start.7
  291.3 10.7 %copy-start.1 = (f32[512,8192]{0,1:T(8,128)S(1)}, f32[512,8192]{0,1:T(8,128)}, u32[]{:S(2)}) copy-start(f32[512,8192]{0,1:T(8,128)} %copy-done) | copy-start | bytes 50331652
  307.7 78.5 %copy-start.6 = (f32[512]{0:T(512)}, f32[512]{0:T(512)S(1)}, u32[]{:S(2)}) copy-start(f32[512]{0:T(512)S(1)} %multiply_select_fusion) | copy-start | bytes 6148
  369.5 12.7 %collective-permute-start.8 = (f32[8,512]{1,0:T(8,128)S(1)}, f32[8,512]{1,0:T(8,128)S(1)}, u32[]{:S(2)}, u32[]{:S(2)}) collective-permute-start(f32[8,512]{1,0:T(8,128)S(1)} %slice_bitcast_fusion.5), channel_id=1, source_target_pairs={{0,8},{8,16},{16,24},{24,0},{1,9},{9,17},{17,25},{25,1},{2,10},{10... | collective-permute-start | bytes 49160 | tf_op jit(solution)/shard_map/ppermute | solution.py:26
  381.3 1.2 collective-permute-start.9
  382.5 3.6 collective-permute-start.10
